TPU v7x, 32 devices: a whole 2x2x4 slice. The times are simulated.
32 devices in a mesh: group: 2 (over y), phi: 4 (over z), eta: 2 (over x), half: 2 (over core).
Axes of the slice: x: 2, y: 2, z: 4, core: 2. Of those that a mesh axis runs over, the one named last changes fastest.
Arguments:
- feats: bfloat16 [8, 2, 512, 512], P(('group', 'phi'), 'eta', 'half'), parts along dimension 0, may hold values from -6 to 6
- cotangent: bfloat16 [8, 2, 512, 512], P(('group', 'phi'), 'eta', 'half'), parts along dimension 0, may hold values from -6 to 6
- tiles: bfloat16 [8, 2, 24, 128, 128], P(('group', 'phi'), 'eta', 'half'), parts along dimension 0, may hold values from -0.21875 to 0.21875
- tile_src: int32 [8, 2, 24], P(('group', 'phi'), 'eta', 'half'), parts along dimension 0, may hold values from 0 to 5
- tile_dst: int32 [8, 2, 24], P(('group', 'phi'), 'eta', 'half'), parts along dimension 0, may hold values from -1 to 3, as said below
- weights: bfloat16 [2, 512, 512], replicated, may hold values from -0.25 to 0.25
- mask: int32 [2, 8, 8], replicated, may hold values 0 or 1
- counts: int32 [8, 2], P(('group', 'phi'), 'eta'), parts along dimension 0, may hold values from 128 to 512, as said below
Outputs:
- final: bfloat16 [8, 2, 512, 512], P(('group', 'phi'), 'eta', 'half'), parts along dimension 0
- grad_w: float32 [4, 512, 512], P('group', 'phi'), parts along dimension 0
There are 2 independent parts, one for each index of `group`. A program takes and returns all parts, laid end to end along the dimension named above; an argument that names none is the same for every part. Nothing has to cross between parts.
Inputs may be any that keep to these rules, and one draw needn't show every extreme that they name: `tile_dst`: in each region half the live tiles fill the first slots and the rest hold -1; some region half has all 12 slots live. `counts`: some region is full and some holds a quarter of its hits.
All inputs are finite; a program needn't handle non-finite values.
Results may differ from a plain program's by a relative error of at most 0.017.
Values may be sent and summed in bfloat16 or wider, within the bound.
No kernel may reach another device: no remote copies, remote signals or barrier semaphores. Data moves between devices by JAX's collectives and lax.ppermute only.
A program may use at most 64 MiB of HBM per device.

v0:
```python
import jax
import jax.numpy as jnp
from jax import lax
from jax.sharding import PartitionSpec as P


def with_halo(block, sides, width, periodic):
    for axis, dim in sides:
        count = lax.axis_size(axis)
        forward = [(i, i + 1) for i in range(count - 1)]
        if periodic:
            forward.append((count - 1, 0))
        backward = [(target, source) for source, target in forward]
        low = lax.ppermute(
            lax.slice_in_dim(block, block.shape[dim] - width, None, axis=dim), axis, forward
        )
        high = lax.ppermute(lax.slice_in_dim(block, 0, width, axis=dim), axis, backward)
        block = jnp.concatenate([low, block, high], axis=dim)
    return block


def silu_slope(pre):
    sigma = jax.nn.sigmoid(pre)
    return sigma * (1.0 + pre * (1.0 - sigma))


def body(feats, cotangent, tiles, tile_src, tile_dst, weights, mask, counts):
    rows = feats.shape[2]
    width = feats.shape[3]
    block = tiles.shape[3]
    own_blocks = rows // block
    halves = lax.axis_size("half")
    region_blocks = own_blocks * halves
    slots = own_blocks + 4
    layers = weights.shape[0]
    grid = mask.shape[1]
    side = width // grid
    tile_set = tiles[0, 0]
    sources_of = tile_src[0, 0]
    targets = tile_dst[0, 0]
    first_row = lax.axis_index("half") * rows
    live = (first_row + jnp.arange(rows, dtype=jnp.int32) < counts[0, 0]).astype(jnp.float32)[
        :, None
    ]
    eta_here = lax.axis_index("eta")
    lower_eta = (eta_here > 0).astype(jnp.bfloat16)
    upper_eta = (eta_here < lax.axis_size("eta") - 1).astype(jnp.bfloat16)
    mask_full = (
        jnp.broadcast_to(mask[:, :, None, :, None], (layers, grid, side, grid, side))
        .reshape(layers, width, width)
        .astype(jnp.float32)
    )
    masked = (weights.astype(jnp.float32) * mask_full).astype(jnp.bfloat16)
    block_ids = jnp.arange(region_blocks, dtype=jnp.int32)
    slot_ids = jnp.arange(slots, dtype=jnp.int32)
    state = feats[0, 0]
    inputs = []
    pres = []
    for layer in range(layers):
        edge = state[:block][None, None]
        padded = with_halo(edge, (("phi", 0), ("eta", 1)), 1, True)
        rims = jnp.stack(
            [padded[0, 1], padded[2, 1], padded[1, 0] * lower_eta, padded[1, 2] * upper_eta]
        )
        messages_picked = jnp.take(
            jnp.concatenate([state.reshape(own_blocks, block, width), rims], axis=0),
            sources_of,
            axis=0,
        )
        messages_parts = jnp.einsum(
            "tij,tjd->tid", tile_set, messages_picked, preferred_element_type=jnp.float32
        )
        messages_onehot = (targets[None, :] == block_ids[:, None]).astype(jnp.float32)
        messages_total = jnp.einsum(
            "bt,tid->bid", messages_onehot, messages_parts, precision=lax.Precision.HIGHEST
        )
        region = messages_total.reshape(region_blocks * block, width)
        gathered = lax.psum_scatter(
            region.astype(jnp.bfloat16), "half", scatter_dimension=0, tiled=True
        ).astype(jnp.float32)
        hfloat = state.astype(jnp.float32)
        mixed = (hfloat + gathered).astype(jnp.bfloat16)
        pre = jnp.dot(mixed, masked[layer], preferred_element_type=jnp.float32)
        state = (live * (hfloat + jax.nn.silu(pre))).astype(jnp.bfloat16)
        inputs.append(mixed)
        pres.append(pre)
    upstream = cotangent[0, 0].astype(jnp.float32)
    partials = [None] * layers
    for layer in reversed(range(layers)):
        delta = (upstream * live * silu_slope(pres[layer])).astype(jnp.bfloat16)
        partials[layer] = (
            jnp.einsum("rd,re->de", inputs[layer], delta, preferred_element_type=jnp.float32)
            * mask_full[layer]
        )
        if layer > 0:
            back = jnp.einsum(
                "re,de->rd", delta, masked[layer], preferred_element_type=jnp.float32
            ).astype(jnp.bfloat16)
            whole = lax.all_gather(back, "half", axis=0, tiled=True)
            valid = (targets >= 0).astype(jnp.bfloat16)
            picked = (
                jnp.take(
                    whole.reshape(region_blocks, block, width), jnp.maximum(targets, 0), axis=0
                )
                * valid[:, None, None]
            )
            parts = jnp.einsum("tji,tjd->tid", tile_set, picked, preferred_element_type=jnp.float32)
            onehot = (sources_of[None, :] == slot_ids[:, None]).astype(jnp.float32)
            total = jnp.einsum("st,tid->sid", onehot, parts, precision=lax.Precision.HIGHEST)
            returned_phi = with_halo(
                total[own_blocks : own_blocks + 2].astype(jnp.bfloat16), (("phi", 0),), 1, True
            ).astype(jnp.float32)
            returned_eta = with_halo(
                total[own_blocks + 2 :].astype(jnp.bfloat16), (("eta", 0),), 1, False
            ).astype(jnp.float32)
            extra = returned_phi[0] + returned_phi[3] + returned_eta[0] + returned_eta[3]
            own = total[:own_blocks].reshape(rows, width)
            own = jnp.concatenate([own[:block] + extra, own[block:]], axis=0)
            upstream = live * upstream + back.astype(jnp.float32) + own
    stacked = jnp.stack(partials)
    shares = lax.psum_scatter(stacked.astype(jnp.bfloat16), "phi", scatter_dimension=1, tiled=True)
    result = lax.psum(shares, ("eta", "half")).astype(jnp.float32)
    return (state[None, None], result)


def solution(mesh):
    in_specs = (
        P(("group", "phi"), "eta", "half", None),
        P(("group", "phi"), "eta", "half", None),
        P(("group", "phi"), "eta", "half", None, None),
        P(("group", "phi"), "eta", "half"),
        P(("group", "phi"), "eta", "half"),
        P(),
        P(),
        P(("group", "phi"), "eta"),
    )
    out_specs = (P(("group", "phi"), "eta", "half", None), P("group", "phi", None))
    return jax.shard_map(body, mesh=mesh, in_specs=in_specs, out_specs=out_specs, check_vma=False)
```

profile of v0, /device:TPU:0, one launch (start us, length us, event | category | flops | bytes accessed | tf_op | source)
XLA Modules:
  0.0 213.0 jit_solution(10340029275667400948)
XLA Ops:
  8.2 3.1 %collective-permute-start = (bf16[1,1,128,512]{3,2,1,0:T(8,128)(2,1)S(1)}, bf16[1,1,128,512]{3,2,1,0:T(8,128)(2,1)S(1)}, u32[]{:S(2)}, u32[]{:S(2)}) collective-permute-start(bf16[1,1,128,512]{3,2,1,0:T(8,128)(2,1)S(1)} %slice.89), channel_id=1, source_target_pairs={{0,4},{4,8},{8,12},{12,0},{1,5},{5,9},{9,13},{13,1},{2,6},{6,10},{... | collective-permute-start | bytes 393224 | tf_op jit(solution)/shard_map/ppermute | solution.py:14
  11.3 2.1 collective-permute-start.1
  15.7 1.9 collective-permute-done
  21.2 10.0 %collective-permute-done.2 = bf16[3,1,128,512]{3,2,1,0:T(8,128)(2,1)S(1)} collective-permute-done((bf16[3,1,128,512]{3,2,1,0:T(8,128)(2,1)S(1)}, bf16[3,1,128,512]{3,2,1,0:T(8,128)(2,1)S(1)}, u32[]{:S(2)}, u32[]{:S(2)}) %collective-permute-start.2) | collective-permute-done | bytes 393248 | tf_op jit(solution)/shard_map/ppermute | solution.py:14
  31.2 6.8 %collective-permute-done.3 = bf16[3,1,128,512]{3,2,1,0:T(8,128)(2,1)S(1)} collective-permute-done((bf16[3,1,128,512]{3,2,1,0:T(8,128)(2,1)S(1)}, bf16[3,1,128,512]{3,2,1,0:T(8,128)(2,1)S(1)}, u32[]{:S(2)}, u32[]{:S(2)}) %collective-permute-start.3) | collective-permute-done | bytes 393248 | tf_op jit(solution)/shard_map/ppermute | solution.py:17
  38.0 1.9 gather_fusion.1
  39.9 2.1 fusion.8
  42.0 3.5 %copy.19 = f32[12,512,128]{1,0,2:T(8,128)} copy(f32[12,512,128]{2,1,0:T(8,128)S(1)} %fusion.8) | data formatting | bytes 6291456 | tf_op jit(solution)/shard_map/tij,tjd->tid/dot_general | solution.py:70
  45.5 3.8 %fusion.16 = bf16[4,128,512]{2,0,1:T(4,128)(2,1)S(1)} fusion(f32[12,512,128]{1,0,2:T(8,128)} %copy.19, s32[12]{0:T(128)S(1)} %bitcast.122), kind=kOutput, calls=%fused_computation.22 | convolution fusion | flops 38010928 | bytes 3670064 | tf_op jit(solution)/shard_map/bt,tid->bid/dot_general | solution.py:74
  50.3 2.3 %broadcast_in_dim.41 = f32[2,8,64,8,64]{4,3,2,1,0:T(8,128)} broadcast(f32[2,8,8]{2,1,0:T(8,128)S(1)} %convert_element_type.115), dimensions={0,1,3} | broadcast | bytes 2097664 | tf_op jit(solution)/shard_map/broadcast_in_dim | solution.py:49
  52.6 3.5 %convert_element_type.116 = f32[2,512,512]{2,1,0:T(8,128)S(1)} reshape(f32[2,8,64,8,64]{4,3,2,1,0:T(8,128)} %broadcast_in_dim.41) | data formatting | bytes 4194304 | tf_op jit(solution)/shard_map/convert_element_type | solution.py:51
  58.7 2.4 %fusion.35 = (bf16[256,512]{1,0:T(8,128)(2,1)S(1)}, f32[256,512]{1,0:T(8,128)}) fusion(bf16[1,1,256,512]{3,2,1,0:T(8,128)(2,1)} %param.10, f32[256]{0:T(256)} %compare_convert_fusion.1, bf16[2,512,512]{2,1,0:T(8,128)(2,1)} %multiply_convert_fusion, bf16[256,512]{1,0:T(8,128)(2,1)} %reduce-scatter.4.cloned.1.call-done), kind=kOutput, calls=%fused_computation.43 | convolution fusion | flops 135790592 | bytes 2098176 | tf_op jit(solution)/shard_map/dot_general | solution.py:83
  62.9 2.1 collective-permute-start.5
  65.0 4.4 %collective-permute-done.4 = bf16[1,1,128,512]{3,2,1,0:T(8,128)(2,1)S(1)} collective-permute-done((bf16[1,1,128,512]{3,2,1,0:T(8,128)(2,1)S(1)}, bf16[1,1,128,512]{3,2,1,0:T(8,128)(2,1)S(1)}, u32[]{:S(2)}, u32[]{:S(2)}) %collective-permute-start.4) | collective-permute-done | bytes 131104 | tf_op jit(solution)/shard_map/ppermute | solution.py:14
  72.6 10.0 %collective-permute-done.6 = bf16[3,1,128,512]{3,2,1,0:T(8,128)(2,1)S(1)} collective-permute-done((bf16[3,1,128,512]{3,2,1,0:T(8,128)(2,1)S(1)}, bf16[3,1,128,512]{3,2,1,0:T(8,128)(2,1)S(1)}, u32[]{:S(2)}, u32[]{:S(2)}) %collective-permute-start.6) | collective-permute-done | bytes 393248 | tf_op jit(solution)/shard_map/ppermute | solution.py:14
  82.7 6.9 %collective-permute-done.7 = bf16[3,1,128,512]{3,2,1,0:T(8,128)(2,1)S(1)} collective-permute-done((bf16[3,1,128,512]{3,2,1,0:T(8,128)(2,1)S(1)}, bf16[3,1,128,512]{3,2,1,0:T(8,128)(2,1)S(1)}, u32[]{:S(2)}, u32[]{:S(2)}) %collective-permute-start.7) | collective-permute-done | bytes 393248 | tf_op jit(solution)/shard_map/ppermute | solution.py:17
  89.6 1.9 gather_fusion.2
  91.5 2.1 fusion.6
  93.6 3.5 %copy.20 = f32[12,512,128]{1,0,2:T(8,128)} copy(f32[12,512,128]{2,1,0:T(8,128)S(1)} %fusion.6) | data formatting | bytes 6291456 | tf_op jit(solution)/shard_map/tij,tjd->tid/dot_general | solution.py:70
  97.1 3.8 %fusion.19 = bf16[4,128,512]{2,0,1:T(4,128)(2,1)S(1)} fusion(f32[12,512,128]{1,0,2:T(8,128)} %copy.20, s32[12]{0:T(128)S(1)} %bitcast.123), kind=kOutput, calls=%fused_computation.23 | convolution fusion | flops 38010928 | bytes 3670064 | tf_op jit(solution)/shard_map/bt,tid->bid/dot_general | solution.py:74
  105.3 4.0 %reduce-scatter.6.cloned.1.call-done = bf16[256,512]{1,0:T(8,128)(2,1)} async-done(((bf16[512,512]{1,0:T(8,128)(2,1)}), bf16[256,512]{1,0:T(8,128)(2,1)}) %reduce-scatter.6.cloned.1.call-update) | async-done | bytes 262160 | tf_op jit(solution)/shard_map/reduce_scatter | solution.py:78
  109.3 2.4 %fusion.42 = (bf16[256,512]{1,0:T(8,128)(2,1)S(1)}, bf16[1,1,256,512]{3,2,1,0:T(8,128)(2,1)}) fusion(bf16[1,1,256,512]{3,2,1,0:T(8,128)(2,1)S(1)} %copy-done.19, f32[256]{0:T(256)S(1)} %copy-done.17, bf16[256,512]{1,0:T(8,128)(2,1)S(1)} %copy-done.3, bf16[2,512,512]{2,1,0:T(8,128)(2,1)} %multiply_convert_fusion, ...), kind=kOutput, calls=%fused_computation.54 | convolution fusion | flops 136839168 | bytes 2098176 | tf_op jit(solution)/shard_map/dot_general | solution.py:83
  112.7 2.3 %all_gather.3 = bf16[512,512]{1,0:T(8,128)(2,1)S(1)} all-gather(bf16[256,512]{1,0:T(8,128)(2,1)S(1)} %convolution_convert_fusion), channel_id=1, replica_groups=mesh['group'=2,'phi'=4,'eta'=2,'half'=2] {'half'}, dimensions={0}, use_global_device_ids=true | all-gather | bytes 786432 | tf_op jit(solution)/shard_map/all_gather | solution.py:99
  115.1 1.9 gather_fusion
  116.9 2.1 %fusion.10 = f32[12,512,128]{2,1,0:T(8,128)S(1)} fusion(bf16[12,128,512]{2,1,0:T(8,128)(2,1)} %gather_fusion, pred[12]{0:T(512)(128)(4,1)S(1)} %get-tuple-element.18, bf16[12]{0:T(256)(128)(2,1)S(1)} %get-tuple-element.17, bf16[1,1,12,128,128]{4,3,2,1,0:T(8,128)(2,1)S(1)} %copy-done), kind=kOutput, calls=%fused_computation.14 | convolution fusion | flops 202899456 | bytes 5111844 | tf_op jit(solution)/shard_map/tji,tjd->tid/dot_general | solution.py:107
  119.1 3.5 %copy.21 = f32[12,512,128]{1,0,2:T(8,128)} copy(f32[12,512,128]{2,1,0:T(8,128)S(1)} %fusion.10) | data formatting | bytes 6291456 | tf_op jit(solution)/shard_map/tji,tjd->tid/dot_general | solution.py:107
  122.6 3.7 %fusion = f32[6,128,512]{2,0,1:T(8,128)S(1)} fusion(f32[12,512,128]{1,0,2:T(8,128)} %copy.21, s32[12]{0:T(128)S(1)} %bitcast.124), kind=kOutput, calls=%fused_computation.3 | convolution fusion | flops 56623176 | bytes 4718640 | tf_op jit(solution)/shard_map/st,tid->sid/dot_general | solution.py:109
  127.4 3.8 %collective-permute-start.10 = (bf16[1,128,512]{2,1,0:T(8,128)(2,1)S(1)}, bf16[1,128,512]{2,1,0:T(8,128)(2,1)S(1)}, u32[]{:S(2)}, u32[]{:S(2)}) collective-permute-start(bf16[1,128,512]{2,1,0:T(8,128)(2,1)S(1)} %get-tuple-element.9), channel_id=1, source_target_pairs={{0,2},{1,3},{4,6},{5,7},{8,10},{9,11},{12,14},{13,15},{16,18},{17,... | collective-permute-start | bytes 393224 | tf_op jit(solution)/shard_map/ppermute | solution.py:14
  134.0 2.3 %collective-permute-start.9 = (bf16[1,128,512]{2,1,0:T(8,128)(2,1)S(1)}, bf16[1,128,512]{2,1,0:T(8,128)(2,1)S(1)}, u32[]{:S(2)}, u32[]{:S(2)}) collective-permute-start(bf16[1,128,512]{2,1,0:T(8,128)(2,1)S(1)} %get-tuple-element.10), channel_id=1, source_target_pairs={{4,0},{8,4},{12,8},{0,12},{5,1},{9,5},{13,9},{1,13},{6,2},{10,6},{... | collective-permute-start | bytes 393224 | tf_op jit(solution)/shard_map/ppermute | solution.py:17
  138.5 2.2 %collective-permute-done.8 = bf16[1,128,512]{2,1,0:T(8,128)(2,1)S(1)} collective-permute-done((bf16[1,128,512]{2,1,0:T(8,128)(2,1)S(1)}, bf16[1,128,512]{2,1,0:T(8,128)(2,1)S(1)}, u32[]{:S(2)}, u32[]{:S(2)}) %collective-permute-start.8) | collective-permute-done | bytes 131104 | tf_op jit(solution)/shard_map/ppermute | solution.py:14
  143.9 27.9 %reduce-scatter.8.cloned.1.call-done = bf16[2,128,512]{2,1,0:T(8,128)(2,1)} async-done(((bf16[2,512,512]{2,1,0:T(8,128)(2,1)}), bf16[2,128,512]{2,1,0:T(8,128)(2,1)}) %reduce-scatter.8.cloned.1.call-update) | async-done | bytes 262160 | tf_op jit(solution)/shard_map/reduce_scatter | solution.py:121
  171.8 32.9 %all-reduce.2.cloned.1.call-done = bf16[2,128,512]{2,1,0:T(8,128)(2,1)} async-done(((bf16[2,128,512]{2,1,0:T(8,128)(2,1)}), bf16[2,128,512]{2,1,0:T(8,128)(2,1)}) %all-reduce.2.cloned.1.call-update) | async-done | bytes 262160 | tf_op jit(solution)/shard_map/psum | solution.py:122
  (106 shorter events, 31.2 us)
Async XLA Ops:
  7.2 32.7 %copy-start = (bf16[1,1,12,128,128]{4,3,2,1,0:T(8,128)(2,1)S(1)}, bf16[1,1,12,128,128]{4,3,2,1,0:T(8,128)(2,1)}, u32[]{:S(2)}) copy-start(bf16[1,1,12,128,128]{4,3,2,1,0:T(8,128)(2,1)} %param.12) | copy-start | bytes 1179652
  7.2 51.5 %reduce-scatter.4.cloned.1.call-start = ((), (), s32[]{:S(2)}) async-start(), calls=%async_computation.3 | async-start | bytes 786432 | tf_op jit(solution)/shard_map/reduce_scatter | solution.py:78
  8.2 9.4 %collective-permute-start = (bf16[1,1,128,512]{3,2,1,0:T(8,128)(2,1)S(1)}, bf16[1,1,128,512]{3,2,1,0:T(8,128)(2,1)S(1)}, u32[]{:S(2)}, u32[]{:S(2)}) collective-permute-start(bf16[1,1,128,512]{3,2,1,0:T(8,128)(2,1)S(1)} %slice.89), channel_id=1, source_target_pairs={{0,4},{4,8},{8,12},{12,0},{1,5},{5,9},{9,13},{13,1},{2,6},{6,10},{... | collective-permute-start | bytes 393224 | tf_op jit(solution)/shard_map/ppermute | solution.py:14
  11.3 7.8 %collective-permute-start.1 = (bf16[1,1,128,512]{3,2,1,0:T(8,128)(2,1)S(1)}, bf16[1,1,128,512]{3,2,1,0:T(8,128)(2,1)S(1)}, u32[]{:S(2)}, u32[]{:S(2)}) collective-permute-start(bf16[1,1,128,512]{3,2,1,0:T(8,128)(2,1)S(1)} %slice.89), channel_id=1, source_target_pairs={{4,0},{8,4},{12,8},{0,12},{5,1},{9,5},{13,9},{1,13},{6,2},{10,6},{... | collective-permute-start | bytes 393224 | tf_op jit(solution)/shard_map/ppermute | solution.py:17
  14.7 25.2 %copy-start.16 = (pred[12]{0:T(512)(128)(4,1)}, pred[12]{0:T(512)(128)(4,1)S(1)}, u32[]{:S(2)}) copy-start(pred[12]{0:T(512)(128)(4,1)S(1)} %compare_and_fusion) | copy-start | bytes 40
  19.1 12.1 %collective-permute-start.2 = (bf16[3,1,128,512]{3,2,1,0:T(8,128)(2,1)S(1)}, bf16[3,1,128,512]{3,2,1,0:T(8,128)(2,1)S(1)}, u32[]{:S(2)}, u32[]{:S(2)}) collective-permute-start(bf16[3,1,128,512]{3,2,1,0:T(8,128)(2,1)S(1)} %pad_maximum_fusion.1), channel_id=1, source_target_pairs={{0,2},{2,0},{1,3},{3,1},{4,6},{6,4},{5,7},{7,5},{8,10},{10,8},{9,1... | collective-permute-start | bytes 1179656 | tf_op jit(solution)/shard_map/ppermute | solution.py:14
  20.6 17.4 %collective-permute-start.3 = (bf16[3,1,128,512]{3,2,1,0:T(8,128)(2,1)S(1)}, bf16[3,1,128,512]{3,2,1,0:T(8,128)(2,1)S(1)}, u32[]{:S(2)}, u32[]{:S(2)}) collective-permute-start(bf16[3,1,128,512]{3,2,1,0:T(8,128)(2,1)S(1)} %pad_maximum_fusion.1), channel_id=1, source_target_pairs={{2,0},{0,2},{3,1},{1,3},{6,4},{4,6},{7,5},{5,7},{10,8},{8,10},{11,... | collective-permute-start | bytes 1179656 | tf_op jit(solution)/shard_map/ppermute | solution.py:17
  50.2 59.1 %reduce-scatter.6.cloned.1.call-start = ((), (), s32[]{:S(2)}) async-start(), calls=%async_computation.4 | async-start | bytes 786432 | tf_op jit(solution)/shard_map/reduce_scatter | solution.py:78
  61.1 21.6 %copy-start.2 = (bf16[256,512]{1,0:T(8,128)(2,1)}, bf16[256,512]{1,0:T(8,128)(2,1)S(1)}, u32[]{:S(2)}) copy-start(bf16[256,512]{1,0:T(8,128)(2,1)S(1)} %get-tuple-element.19) | copy-start | bytes 786436
  61.1 8.3 %collective-permute-start.4 = (bf16[1,1,128,512]{3,2,1,0:T(8,128)(2,1)S(1)}, bf16[1,1,128,512]{3,2,1,0:T(8,128)(2,1)S(1)}, u32[]{:S(2)}, u32[]{:S(2)}) collective-permute-start(bf16[1,1,128,512]{3,2,1,0:T(8,128)(2,1)S(1)} %slice_bitcast_fusion.6), channel_id=1, source_target_pairs={{0,4},{4,8},{8,12},{12,0},{1,5},{5,9},{9,13},{13,1},{2,6},{6,10},{... | collective-permute-start | bytes 393224 | tf_op jit(solution)/shard_map/ppermute | solution.py:14
  62.9 7.6 %collective-permute-start.5 = (bf16[1,1,128,512]{3,2,1,0:T(8,128)(2,1)S(1)}, bf16[1,1,128,512]{3,2,1,0:T(8,128)(2,1)S(1)}, u32[]{:S(2)}, u32[]{:S(2)}) collective-permute-start(bf16[1,1,128,512]{3,2,1,0:T(8,128)(2,1)S(1)} %slice_bitcast_fusion.6), channel_id=1, source_target_pairs={{4,0},{8,4},{12,8},{0,12},{5,1},{9,5},{13,9},{1,13},{6,2},{10,6},{... | collective-permute-start | bytes 393224 | tf_op jit(solution)/shard_map/ppermute | solution.py:17
  70.5 12.1 %collective-permute-start.6 = (bf16[3,1,128,512]{3,2,1,0:T(8,128)(2,1)S(1)}, bf16[3,1,128,512]{3,2,1,0:T(8,128)(2,1)S(1)}, u32[]{:S(2)}, u32[]{:S(2)}) collective-permute-start(bf16[3,1,128,512]{3,2,1,0:T(8,128)(2,1)S(1)} %pad_maximum_fusion.2), channel_id=1, source_target_pairs={{0,2},{2,0},{1,3},{3,1},{4,6},{6,4},{5,7},{7,5},{8,10},{10,8},{9,1... | collective-permute-start | bytes 1179656 | tf_op jit(solution)/shard_map/ppermute | solution.py:14
  72.0 17.5 %collective-permute-start.7 = (bf16[3,1,128,512]{3,2,1,0:T(8,128)(2,1)S(1)}, bf16[3,1,128,512]{3,2,1,0:T(8,128)(2,1)S(1)}, u32[]{:S(2)}, u32[]{:S(2)}) collective-permute-start(bf16[3,1,128,512]{3,2,1,0:T(8,128)(2,1)S(1)} %pad_maximum_fusion.2), channel_id=1, source_target_pairs={{2,0},{0,2},{3,1},{1,3},{6,4},{4,6},{7,5},{5,7},{10,8},{8,10},{11,... | collective-permute-start | bytes 1179656 | tf_op jit(solution)/shard_map/ppermute | solution.py:17
  101.8 70.0 %reduce-scatter.8.cloned.1.call-start = ((), (), s32[]{:S(2)}) async-start(), calls=%async_computation.5 | async-start | bytes 1310720 | tf_op jit(solution)/shard_map/reduce_scatter | solution.py:121
  103.7 5.6 %copy-start.3 = (bf16[256,512]{1,0:T(8,128)(2,1)S(1)}, bf16[256,512]{1,0:T(8,128)(2,1)}, u32[]{:S(2)}) copy-start(bf16[256,512]{1,0:T(8,128)(2,1)} %copy-done.2) | copy-start | bytes 786436
  103.7 5.6 %copy-start.17 = (f32[256]{0:T(256)S(1)}, f32[256]{0:T(256)}, u32[]{:S(2)}) copy-start(f32[256]{0:T(256)} %compare_convert_fusion.1) | copy-start | bytes 3076
  103.7 5.6 %copy-start.19 = (bf16[1,1,256,512]{3,2,1,0:T(8,128)(2,1)S(1)}, bf16[1,1,256,512]{3,2,1,0:T(8,128)(2,1)}, u32[]{:S(2)}) copy-start(bf16[1,1,256,512]{3,2,1,0:T(8,128)(2,1)} %param.11) | copy-start | bytes 786436
  105.2 6.4 %copy-start.7 = (bf16[2,512,512]{2,1,0:T(8,128)(2,1)S(1)}, bf16[2,512,512]{2,1,0:T(8,128)(2,1)}, u32[]{:S(2)}) copy-start(bf16[2,512,512]{2,1,0:T(8,128)(2,1)} %multiply_convert_fusion) | copy-start | bytes 3145732
  127.3 9.1 %copy-start.1 = (f32[512,512]{1,0:T(8,128)S(1)}, f32[512,512]{1,0:T(8,128)}, u32[]{:S(2)}) copy-start(f32[512,512]{1,0:T(8,128)} %squeeze.39) | copy-start | bytes 3145732
  127.3 9.1 %copy-start.4 = (bf16[256,512]{1,0:T(8,128)(2,1)S(1)}, bf16[256,512]{1,0:T(8,128)(2,1)}, u32[]{:S(2)}) copy-start(bf16[256,512]{1,0:T(8,128)(2,1)} %copy-done.2) | copy-start | bytes 786436
  127.3 9.1 %copy-start.11 = (bf16[256,512]{1,0:T(8,128)(2,1)S(1)}, bf16[256,512]{1,0:T(8,128)(2,1)}, u32[]{:S(2)}) copy-start(bf16[256,512]{1,0:T(8,128)(2,1)} %reduce-scatter.6.cloned.1.call-done) | copy-start | bytes 786436
  127.3 9.0 %copy-start.13 = (bf16[256,512]{1,0:T(8,128)(2,1)S(1)}, bf16[256,512]{1,0:T(8,128)(2,1)}, u32[]{:S(2)}) copy-start(bf16[256,512]{1,0:T(8,128)(2,1)} %copy-done.12) | copy-start | bytes 786436
  127.4 9.4 %collective-permute-start.10 = (bf16[1,128,512]{2,1,0:T(8,128)(2,1)S(1)}, bf16[1,128,512]{2,1,0:T(8,128)(2,1)S(1)}, u32[]{:S(2)}, u32[]{:S(2)}) collective-permute-start(bf16[1,128,512]{2,1,0:T(8,128)(2,1)S(1)} %get-tuple-element.9), channel_id=1, source_target_pairs={{0,2},{1,3},{4,6},{5,7},{8,10},{9,11},{12,14},{13,15},{16,18},{17,... | collective-permute-start | bytes 393224 | tf_op jit(solution)/shard_map/ppermute | solution.py:14
  131.1 7.3 %collective-permute-start.11 = (bf16[1,128,512]{2,1,0:T(8,128)(2,1)S(1)}, bf16[1,128,512]{2,1,0:T(8,128)(2,1)S(1)}, u32[]{:S(2)}, u32[]{:S(2)}) collective-permute-start(bf16[1,128,512]{2,1,0:T(8,128)(2,1)S(1)} %get-tuple-element.8), channel_id=1, source_target_pairs={{2,0},{3,1},{6,4},{7,5},{10,8},{11,9},{14,12},{15,13},{18,16},{19,... | collective-permute-start | bytes 393224 | tf_op jit(solution)/shard_map/ppermute | solution.py:17
  132.4 8.2 %collective-permute-start.8 = (bf16[1,128,512]{2,1,0:T(8,128)(2,1)S(1)}, bf16[1,128,512]{2,1,0:T(8,128)(2,1)S(1)}, u32[]{:S(2)}, u32[]{:S(2)}) collective-permute-start(bf16[1,128,512]{2,1,0:T(8,128)(2,1)S(1)} %get-tuple-element.7), channel_id=1, source_target_pairs={{0,4},{4,8},{8,12},{12,0},{1,5},{5,9},{9,13},{13,1},{2,6},{6,10},{... | collective-permute-start | bytes 393224 | tf_op jit(solution)/shard_map/ppermute | solution.py:14
  134.0 8.0 %collective-permute-start.9 = (bf16[1,128,512]{2,1,0:T(8,128)(2,1)S(1)}, bf16[1,128,512]{2,1,0:T(8,128)(2,1)S(1)}, u32[]{:S(2)}, u32[]{:S(2)}) collective-permute-start(bf16[1,128,512]{2,1,0:T(8,128)(2,1)S(1)} %get-tuple-element.10), channel_id=1, source_target_pairs={{4,0},{8,4},{12,8},{0,12},{5,1},{9,5},{13,9},{1,13},{6,2},{10,6},{... | collective-permute-start | bytes 393224 | tf_op jit(solution)/shard_map/ppermute | solution.py:17
  136.3 5.7 %copy-start.22 = (f32[256,512]{1,0:T(8,128)S(1)}, f32[256,512]{1,0:T(8,128)}, u32[]{:S(2)}) copy-start(f32[256,512]{1,0:T(8,128)} %get-tuple-element.20) | copy-start | bytes 1572868
  136.7 5.4 %copy-start.5 = (f32[512,512]{1,0:T(8,128)S(1)}, f32[512,512]{1,0:T(8,128)}, u32[]{:S(2)}) copy-start(f32[512,512]{1,0:T(8,128)} %squeeze.38) | copy-start | bytes 3145732
  136.7 5.4 %copy-start.8 = (bf16[1,1,256,512]{3,2,1,0:T(8,128)(2,1)S(1)}, bf16[1,1,256,512]{3,2,1,0:T(8,128)(2,1)}, u32[]{:S(2)}) copy-start(bf16[1,1,256,512]{3,2,1,0:T(8,128)(2,1)} %param.10) | copy-start | bytes 786436
  136.7 5.4 %copy-start.10 = (bf16[256,512]{1,0:T(8,128)(2,1)S(1)}, bf16[256,512]{1,0:T(8,128)(2,1)}, u32[]{:S(2)}) copy-start(bf16[256,512]{1,0:T(8,128)(2,1)} %copy-done.9) | copy-start | bytes 786436
  136.7 5.4 %copy-start.20 = (bf16[1,1,256,512]{3,2,1,0:T(8,128)(2,1)S(1)}, bf16[1,1,256,512]{3,2,1,0:T(8,128)(2,1)}, u32[]{:S(2)}) copy-start(bf16[1,1,256,512]{3,2,1,0:T(8,128)(2,1)} %param.11) | copy-start | bytes 786436
  143.8 60.8 %all-reduce.2.cloned.1.call-start = ((), (), s32[]{:S(2)}) async-start(), calls=%async_computation.6 | async-start | bytes 524288 | tf_op jit(solution)/shard_map/psum | solution.py:122
  (7 other events, 24.0 us)
Sparse Core Ops, SparseCore 0:
  50.3 7.6 reduce-scatter.3
  101.9 7.3 reduce-scatter.5
  143.9 27.7 reduce-scatter.7
  174.0 30.5 all-reduce.1
where the time goes:
time: 214 us; the launch traced here: 213 us
  waiting for transfers between devices  113 us (53%)
  local copies, waits for them, and re-layouts  29.8 us (14%)
  matrix products  23.7 us (11%)
  starting transfers between devices  22.3 us (10%)
  between operations  14.9 us (7%)
  other arithmetic  7.39 us (3%)
  blocking collectives  2.35 us (1%)
    psum x1, waiting for transfers between devices, body(): result = lax.psum(shares, ('eta', 'half')).astype(jnp.float32)  32.9 us
    ppermute x6, waiting for transfers between devices, with_halo(): lax.ppermute(lax.slice_in_dim(block, block.shape[dim] - width, None, axis...  28.5 us
    reduce_scatter x1, waiting for transfers between devices, body(): lax.psum_scatter(stacked.astype(jnp.bfloat16), 'phi', scatter_dimension=1...  27.9 us
    ppermute x6, waiting for transfers between devices, with_halo(): lax.ppermute(lax.slice_in_dim(block, 0, width, axis=dim), axis, backward)  19.2 us
    ppermute x6, starting transfers between devices, with_halo(): lax.ppermute(lax.slice_in_dim(block, block.shape[dim] - width, None, axis...  13.3 us
    ppermute x6, starting transfers between devices, with_halo(): lax.ppermute(lax.slice_in_dim(block, 0, width, axis=dim), axis, backward)  8.89 us
    dot_general x2, matrix products, body(): jnp.einsum('bt,tid->bid', messages_onehot, messages_parts, precision=lax....  7.58 us
    dot_general x2, local copies, waits for them, and re-layouts, body(): jnp.einsum('tij,tjd->tid', tile_set, messages_picked, preferred_element_t...  6.92 us
  transfers between devices with their start and end apart: 16, of which 14 were waited for; matrix products, arithmetic and copies ran while one was open for 7% of the time, Pallas kernels for 0%

commit v1 on v0

--- a/solution.py
+++ b/solution.py
@@ -119,7 +119,7 @@
             upstream = live * upstream + back.astype(jnp.float32) + own
     stacked = jnp.stack(partials)
     shares = lax.psum_scatter(stacked.astype(jnp.bfloat16), "phi", scatter_dimension=1, tiled=True)
-    result = lax.psum(shares, ("eta", "half")).astype(jnp.float32)
+    result = jnp.sum(lax.all_gather(shares, ("eta", "half")), axis=0).astype(jnp.float32)
     return (state[None, None], result)
 
 

time: 214 us -> 198 us (0.925)
  waiting for transfers between devices: 113 us -> 96.5 us
    psum x1 -> x0, waiting for transfers between devices: 32.9 us -> none  [body(): result = lax.psum(shares, ('eta', 'half')).astype(jnp.float32)]
    all_gather x0 -> x1, waiting for transfers between devices: none -> 16.9 us  [body(): lax.all_gather(shares, ('eta', 'half'))]
where the time goes in v1:
time: 198 us; the launch traced here: 197 us
  waiting for transfers between devices  96.5 us (49%)
  local copies, waits for them, and re-layouts  29.8 us (15%)
  matrix products  23.7 us (12%)
  starting transfers between devices  22.3 us (11%)
  between operations  14.9 us (8%)
  other arithmetic  7.9 us (4%)
  blocking collectives  2.35 us (1%)
    ppermute x6, waiting for transfers between devices, with_halo(): lax.ppermute(lax.slice_in_dim(block, block.shape[dim] - width, None, axis...  28.5 us
    reduce_scatter x1, waiting for transfers between devices, body(): lax.psum_scatter(stacked.astype(jnp.bfloat16), 'phi', scatter_dimension=1...  27.9 us
    ppermute x6, waiting for transfers between devices, with_halo(): lax.ppermute(lax.slice_in_dim(block, 0, width, axis=dim), axis, backward)  19.2 us
    all_gather x1, waiting for transfers between devices, body(): lax.all_gather(shares, ('eta', 'half'))  16.9 us
    ppermute x6, starting transfers between devices, with_halo(): lax.ppermute(lax.slice_in_dim(block, block.shape[dim] - width, None, axis...  13.3 us
    ppermute x6, starting transfers between devices, with_halo(): lax.ppermute(lax.slice_in_dim(block, 0, width, axis=dim), axis, backward)  8.89 us
    dot_general x2, matrix products, body(): jnp.einsum('bt,tid->bid', messages_onehot, messages_parts, precision=lax....  7.58 us
    dot_general x2, local copies, waits for them, and re-layouts, body(): jnp.einsum('tij,tjd->tid', tile_set, messages_picked, preferred_element_t...  6.92 us
  transfers between devices with their start and end apart: 16, of which 14 were waited for; matrix products, arithmetic and copies ran while one was open for 7% of the time, Pallas kernels for 0%

profile of v1, /device:TPU:0, one launch (start us, length us, event | category | flops | bytes accessed | tf_op | source)
XLA Modules:
  0.0 197.5 jit_solution(15014988691890425276)
XLA Ops:
  8.2 3.1 %collective-permute-start = (bf16[1,1,128,512]{3,2,1,0:T(8,128)(2,1)S(1)}, bf16[1,1,128,512]{3,2,1,0:T(8,128)(2,1)S(1)}, u32[]{:S(2)}, u32[]{:S(2)}) collective-permute-start(bf16[1,1,128,512]{3,2,1,0:T(8,128)(2,1)S(1)} %slice.89), channel_id=1, source_target_pairs={{0,4},{4,8},{8,12},{12,0},{1,5},{5,9},{9,13},{13,1},{2,6},{6,10},{... | collective-permute-start | bytes 393224 | tf_op jit(solution)/shard_map/ppermute | solution.py:14
  11.3 2.1 %collective-permute-start.1 = (bf16[1,1,128,512]{3,2,1,0:T(8,128)(2,1)S(1)}, bf16[1,1,128,512]{3,2,1,0:T(8,128)(2,1)S(1)}, u32[]{:S(2)}, u32[]{:S(2)}) collective-permute-start(bf16[1,1,128,512]{3,2,1,0:T(8,128)(2,1)S(1)} %slice.89), channel_id=1, source_target_pairs={{4,0},{8,4},{12,8},{0,12},{5,1},{9,5},{13,9},{1,13},{6,2},{10,6},{... | collective-permute-start | bytes 393224 | tf_op jit(solution)/shard_map/ppermute | solution.py:17
  15.7 1.9 collective-permute-done
  21.2 10.0 %collective-permute-done.2 = bf16[3,1,128,512]{3,2,1,0:T(8,128)(2,1)S(1)} collective-permute-done((bf16[3,1,128,512]{3,2,1,0:T(8,128)(2,1)S(1)}, bf16[3,1,128,512]{3,2,1,0:T(8,128)(2,1)S(1)}, u32[]{:S(2)}, u32[]{:S(2)}) %collective-permute-start.2) | collective-permute-done | bytes 393248 | tf_op jit(solution)/shard_map/ppermute | solution.py:14
  31.2 6.8 %collective-permute-done.3 = bf16[3,1,128,512]{3,2,1,0:T(8,128)(2,1)S(1)} collective-permute-done((bf16[3,1,128,512]{3,2,1,0:T(8,128)(2,1)S(1)}, bf16[3,1,128,512]{3,2,1,0:T(8,128)(2,1)S(1)}, u32[]{:S(2)}, u32[]{:S(2)}) %collective-permute-start.3) | collective-permute-done | bytes 393248 | tf_op jit(solution)/shard_map/ppermute | solution.py:17
  38.0 1.9 gather_fusion.1
  39.9 2.1 %convolution_bitcast_fusion.2 = f32[12,128,512]{1,2,0:T(8,128)S(1)} fusion(bf16[12,128,512]{2,1,0:T(8,128)(2,1)} %gather_fusion.1, pred[12]{0:T(512)(128)(4,1)S(1)} %compare_and_fusion, bf16[1,1,12,128,128]{4,3,2,1,0:T(8,128)(2,1)S(1)} %copy-done), kind=kOutput, calls=%fused_computation.6 | convolution fusion | flops 202113024 | bytes 5111820 | tf_op jit(solution)/shard_map/tij,tjd->tid/dot_general | solution.py:70
  42.0 3.5 %copy.28 = f32[12,128,512]{2,0,1:T(8,128)} copy(f32[12,128,512]{1,2,0:T(8,128)S(1)} %convolution_bitcast_fusion.2) | data formatting | bytes 6291456 | tf_op jit(solution)/shard_map/tij,tjd->tid/dot_general | solution.py:70
  45.5 3.8 %convolution_convert_fusion.1 = bf16[4,128,512]{2,0,1:T(4,128)(2,1)S(1)} fusion(f32[12,128,512]{2,0,1:T(8,128)} %copy.28, s32[12]{0:T(128)S(1)} %bitcast.120), kind=kOutput, calls=%fused_computation.17 | convolution fusion | flops 38010928 | bytes 3670064 | tf_op jit(solution)/shard_map/bt,tid->bid/dot_general | solution.py:74
  50.3 2.3 %broadcast_in_dim.41 = f32[2,8,64,8,64]{4,3,2,1,0:T(8,128)} broadcast(f32[2,8,8]{2,1,0:T(8,128)S(1)} %convert_element_type.117), dimensions={0,1,3} | broadcast | bytes 2097664 | tf_op jit(solution)/shard_map/broadcast_in_dim | solution.py:49
  52.6 3.5 %convert_element_type.118 = f32[2,512,512]{2,1,0:T(8,128)S(1)} reshape(f32[2,8,64,8,64]{4,3,2,1,0:T(8,128)} %broadcast_in_dim.41) | data formatting | bytes 4194304 | tf_op jit(solution)/shard_map/convert_element_type | solution.py:51
  58.7 2.4 %fusion.20 = (bf16[256,512]{1,0:T(8,128)(2,1)S(1)}, f32[256,512]{1,0:T(8,128)}) fusion(bf16[1,1,256,512]{3,2,1,0:T(8,128)(2,1)} %param.10, f32[256]{0:T(256)} %compare_convert_fusion.1, bf16[2,512,512]{2,1,0:T(8,128)(2,1)} %multiply_convert_fusion, bf16[256,512]{1,0:T(8,128)(2,1)} %reduce-scatter.4.cloned.1.call-done), kind=kOutput, calls=%fused_computation.37 | convolution fusion | flops 135790592 | bytes 2098176 | tf_op jit(solution)/shard_map/dot_general | solution.py:83
  62.9 2.1 %collective-permute-start.5 = (bf16[1,1,128,512]{3,2,1,0:T(8,128)(2,1)S(1)}, bf16[1,1,128,512]{3,2,1,0:T(8,128)(2,1)S(1)}, u32[]{:S(2)}, u32[]{:S(2)}) collective-permute-start(bf16[1,1,128,512]{3,2,1,0:T(8,128)(2,1)S(1)} %slice_bitcast_fusion.6), channel_id=1, source_target_pairs={{4,0},{8,4},{12,8},{0,12},{5,1},{9,5},{13,9},{1,13},{6,2},{10,6},{... | collective-permute-start | bytes 393224 | tf_op jit(solution)/shard_map/ppermute | solution.py:17
  65.0 4.4 %collective-permute-done.4 = bf16[1,1,128,512]{3,2,1,0:T(8,128)(2,1)S(1)} collective-permute-done((bf16[1,1,128,512]{3,2,1,0:T(8,128)(2,1)S(1)}, bf16[1,1,128,512]{3,2,1,0:T(8,128)(2,1)S(1)}, u32[]{:S(2)}, u32[]{:S(2)}) %collective-permute-start.4) | collective-permute-done | bytes 131104 | tf_op jit(solution)/shard_map/ppermute | solution.py:14
  72.6 10.0 %collective-permute-done.6 = bf16[3,1,128,512]{3,2,1,0:T(8,128)(2,1)S(1)} collective-permute-done((bf16[3,1,128,512]{3,2,1,0:T(8,128)(2,1)S(1)}, bf16[3,1,128,512]{3,2,1,0:T(8,128)(2,1)S(1)}, u32[]{:S(2)}, u32[]{:S(2)}) %collective-permute-start.6) | collective-permute-done | bytes 393248 | tf_op jit(solution)/shard_map/ppermute | solution.py:14
  82.7 6.9 %collective-permute-done.7 = bf16[3,1,128,512]{3,2,1,0:T(8,128)(2,1)S(1)} collective-permute-done((bf16[3,1,128,512]{3,2,1,0:T(8,128)(2,1)S(1)}, bf16[3,1,128,512]{3,2,1,0:T(8,128)(2,1)S(1)}, u32[]{:S(2)}, u32[]{:S(2)}) %collective-permute-start.7) | collective-permute-done | bytes 393248 | tf_op jit(solution)/shard_map/ppermute | solution.py:17
  89.6 1.9 gather_fusion.2
  91.5 2.1 %convolution_bitcast_fusion.1 = f32[12,128,512]{1,2,0:T(8,128)S(1)} fusion(bf16[12,128,512]{2,1,0:T(8,128)(2,1)} %gather_fusion.2, pred[12]{0:T(512)(128)(4,1)} %copy-done.16, bf16[1,1,12,128,128]{4,3,2,1,0:T(8,128)(2,1)S(1)} %copy-done), kind=kOutput, calls=%fused_computation.5 | convolution fusion | flops 202113024 | bytes 5111820 | tf_op jit(solution)/shard_map/tij,tjd->tid/dot_general | solution.py:70
  93.6 3.5 %copy.31 = f32[12,128,512]{2,0,1:T(8,128)} copy(f32[12,128,512]{1,2,0:T(8,128)S(1)} %convolution_bitcast_fusion.1) | data formatting | bytes 6291456 | tf_op jit(solution)/shard_map/tij,tjd->tid/dot_general | solution.py:70
  97.1 3.8 %convolution_convert_fusion = bf16[4,128,512]{2,0,1:T(4,128)(2,1)S(1)} fusion(f32[12,128,512]{2,0,1:T(8,128)} %copy.31, s32[12]{0:T(128)S(1)} %bitcast.121), kind=kOutput, calls=%fused_computation.16 | convolution fusion | flops 38010928 | bytes 3670064 | tf_op jit(solution)/shard_map/bt,tid->bid/dot_general | solution.py:74
  105.3 4.0 %reduce-scatter.6.cloned.1.call-done = bf16[256,512]{1,0:T(8,128)(2,1)} async-done(((bf16[512,512]{1,0:T(8,128)(2,1)}), bf16[256,512]{1,0:T(8,128)(2,1)}) %reduce-scatter.6.cloned.1.call-update) | async-done | bytes 262160 | tf_op jit(solution)/shard_map/reduce_scatter | solution.py:78
  109.3 2.4 %fusion.27 = (bf16[256,512]{1,0:T(8,128)(2,1)S(1)}, bf16[1,1,256,512]{3,2,1,0:T(8,128)(2,1)}) fusion(bf16[1,1,256,512]{3,2,1,0:T(8,128)(2,1)S(1)} %copy-done.19, f32[256]{0:T(256)S(1)} %copy-done.17, bf16[256,512]{1,0:T(8,128)(2,1)S(1)} %copy-done.3, bf16[2,512,512]{2,1,0:T(8,128)(2,1)} %multiply_convert_fusion, ...), kind=kOutput, calls=%fused_computation.48 | convolution fusion | flops 136839168 | bytes 2098176 | tf_op jit(solution)/shard_map/dot_general | solution.py:83
  112.7 2.3 %all_gather.9 = bf16[512,512]{1,0:T(8,128)(2,1)S(1)} all-gather(bf16[256,512]{1,0:T(8,128)(2,1)S(1)} %convolution_convert_fusion.2), channel_id=1, replica_groups=mesh['group'=2,'phi'=4,'eta'=2,'half'=2] {'half'}, dimensions={0}, use_global_device_ids=true | all-gather | bytes 786432 | tf_op jit(solution)/shard_map/all_gather | solution.py:99
  115.1 1.9 gather_fusion
  116.9 2.1 %convolution_bitcast_fusion = f32[12,128,512]{1,2,0:T(8,128)S(1)} fusion(bf16[12,128,512]{2,1,0:T(8,128)(2,1)} %gather_fusion, pred[12]{0:T(512)(128)(4,1)S(1)} %get-tuple-element.18, bf16[12]{0:T(256)(128)(2,1)S(1)} %get-tuple-element.17, bf16[1,1,12,128,128]{4,3,2,1,0:T(8,128)(2,1)S(1)} %copy-done), kind=kOutput, calls=%fused_computation.4 | convolution fusion | flops 202899456 | bytes 5111844 | tf_op jit(solution)/shard_map/tji,tjd->tid/dot_general | solution.py:107
  119.1 3.5 %copy.34 = f32[12,128,512]{2,0,1:T(8,128)} copy(f32[12,128,512]{1,2,0:T(8,128)S(1)} %convolution_bitcast_fusion) | data formatting | bytes 6291456 | tf_op jit(solution)/shard_map/tji,tjd->tid/dot_general | solution.py:107
  122.6 3.7 %fusion.53 = f32[6,128,512]{2,0,1:T(8,128)S(1)} fusion(f32[12,128,512]{2,0,1:T(8,128)} %copy.34, s32[12]{0:T(128)S(1)} %bitcast.122), kind=kOutput, calls=%fused_computation.96 | convolution fusion | flops 56623176 | bytes 4718640 | tf_op jit(solution)/shard_map/st,tid->sid/dot_general | solution.py:109
  127.4 3.8 %collective-permute-start.10 = (bf16[1,128,512]{2,1,0:T(8,128)(2,1)S(1)}, bf16[1,128,512]{2,1,0:T(8,128)(2,1)S(1)}, u32[]{:S(2)}, u32[]{:S(2)}) collective-permute-start(bf16[1,128,512]{2,1,0:T(8,128)(2,1)S(1)} %get-tuple-element.9), channel_id=1, source_target_pairs={{0,2},{1,3},{4,6},{5,7},{8,10},{9,11},{12,14},{13,15},{16,18},{17,... | collective-permute-start | bytes 393224 | tf_op jit(solution)/shard_map/ppermute | solution.py:14
  134.0 2.3 %collective-permute-start.9 = (bf16[1,128,512]{2,1,0:T(8,128)(2,1)S(1)}, bf16[1,128,512]{2,1,0:T(8,128)(2,1)S(1)}, u32[]{:S(2)}, u32[]{:S(2)}) collective-permute-start(bf16[1,128,512]{2,1,0:T(8,128)(2,1)S(1)} %get-tuple-element.10), channel_id=1, source_target_pairs={{4,0},{8,4},{12,8},{0,12},{5,1},{9,5},{13,9},{1,13},{6,2},{10,6},{... | collective-permute-start | bytes 393224 | tf_op jit(solution)/shard_map/ppermute | solution.py:17
  138.5 2.2 %collective-permute-done.8 = bf16[1,128,512]{2,1,0:T(8,128)(2,1)S(1)} collective-permute-done((bf16[1,128,512]{2,1,0:T(8,128)(2,1)S(1)}, bf16[1,128,512]{2,1,0:T(8,128)(2,1)S(1)}, u32[]{:S(2)}, u32[]{:S(2)}) %collective-permute-start.8) | collective-permute-done | bytes 131104 | tf_op jit(solution)/shard_map/ppermute | solution.py:14
  143.9 27.9 %reduce-scatter.8.cloned.1.call-done = bf16[2,128,512]{2,1,0:T(8,128)(2,1)} async-done(((bf16[2,512,512]{2,1,0:T(8,128)(2,1)}), bf16[2,128,512]{2,1,0:T(8,128)(2,1)}) %reduce-scatter.8.cloned.1.call-update) | async-done | bytes 262160 | tf_op jit(solution)/shard_map/reduce_scatter | solution.py:121
  171.8 16.9 %all-gather.3.cloned.1.call-done = bf16[8,128,512]{2,1,0:T(8,128)(2,1)} async-done(((bf16[2,128,512]{2,1,0:T(8,128)(2,1)}), bf16[8,128,512]{2,1,0:T(8,128)(2,1)}) %all-gather.3.cloned.1.call-update) | async-done | bytes 1048592 | tf_op jit(solution)/shard_map/all_gather | solution.py:122
  (107 shorter events, 31.7 us)
Async XLA Ops:
  7.2 32.7 %copy-start = (bf16[1,1,12,128,128]{4,3,2,1,0:T(8,128)(2,1)S(1)}, bf16[1,1,12,128,128]{4,3,2,1,0:T(8,128)(2,1)}, u32[]{:S(2)}) copy-start(bf16[1,1,12,128,128]{4,3,2,1,0:T(8,128)(2,1)} %param.12) | copy-start | bytes 1179652
  7.2 51.5 %reduce-scatter.4.cloned.1.call-start = ((), (), s32[]{:S(2)}) async-start(), calls=%async_computation.3 | async-start | bytes 786432 | tf_op jit(solution)/shard_map/reduce_scatter | solution.py:78
  8.2 9.4 %collective-permute-start = (bf16[1,1,128,512]{3,2,1,0:T(8,128)(2,1)S(1)}, bf16[1,1,128,512]{3,2,1,0:T(8,128)(2,1)S(1)}, u32[]{:S(2)}, u32[]{:S(2)}) collective-permute-start(bf16[1,1,128,512]{3,2,1,0:T(8,128)(2,1)S(1)} %slice.89), channel_id=1, source_target_pairs={{0,4},{4,8},{8,12},{12,0},{1,5},{5,9},{9,13},{13,1},{2,6},{6,10},{... | collective-permute-start | bytes 393224 | tf_op jit(solution)/shard_map/ppermute | solution.py:14
  11.3 7.8 %collective-permute-start.1 = (bf16[1,1,128,512]{3,2,1,0:T(8,128)(2,1)S(1)}, bf16[1,1,128,512]{3,2,1,0:T(8,128)(2,1)S(1)}, u32[]{:S(2)}, u32[]{:S(2)}) collective-permute-start(bf16[1,1,128,512]{3,2,1,0:T(8,128)(2,1)S(1)} %slice.89), channel_id=1, source_target_pairs={{4,0},{8,4},{12,8},{0,12},{5,1},{9,5},{13,9},{1,13},{6,2},{10,6},{... | collective-permute-start | bytes 393224 | tf_op jit(solution)/shard_map/ppermute | solution.py:17
  14.7 25.2 %copy-start.16 = (pred[12]{0:T(512)(128)(4,1)}, pred[12]{0:T(512)(128)(4,1)S(1)}, u32[]{:S(2)}) copy-start(pred[12]{0:T(512)(128)(4,1)S(1)} %compare_and_fusion) | copy-start | bytes 40
  19.1 12.1 %collective-permute-start.2 = (bf16[3,1,128,512]{3,2,1,0:T(8,128)(2,1)S(1)}, bf16[3,1,128,512]{3,2,1,0:T(8,128)(2,1)S(1)}, u32[]{:S(2)}, u32[]{:S(2)}) collective-permute-start(bf16[3,1,128,512]{3,2,1,0:T(8,128)(2,1)S(1)} %pad_maximum_fusion.1), channel_id=1, source_target_pairs={{0,2},{2,0},{1,3},{3,1},{4,6},{6,4},{5,7},{7,5},{8,10},{10,8},{9,1... | collective-permute-start | bytes 1179656 | tf_op jit(solution)/shard_map/ppermute | solution.py:14
  20.6 17.4 %collective-permute-start.3 = (bf16[3,1,128,512]{3,2,1,0:T(8,128)(2,1)S(1)}, bf16[3,1,128,512]{3,2,1,0:T(8,128)(2,1)S(1)}, u32[]{:S(2)}, u32[]{:S(2)}) collective-permute-start(bf16[3,1,128,512]{3,2,1,0:T(8,128)(2,1)S(1)} %pad_maximum_fusion.1), channel_id=1, source_target_pairs={{2,0},{0,2},{3,1},{1,3},{6,4},{4,6},{7,5},{5,7},{10,8},{8,10},{11,... | collective-permute-start | bytes 1179656 | tf_op jit(solution)/shard_map/ppermute | solution.py:17
  50.2 59.1 %reduce-scatter.6.cloned.1.call-start = ((), (), s32[]{:S(2)}) async-start(), calls=%async_computation.4 | async-start | bytes 786432 | tf_op jit(solution)/shard_map/reduce_scatter | solution.py:78
  61.1 21.6 %copy-start.2 = (bf16[256,512]{1,0:T(8,128)(2,1)}, bf16[256,512]{1,0:T(8,128)(2,1)S(1)}, u32[]{:S(2)}) copy-start(bf16[256,512]{1,0:T(8,128)(2,1)S(1)} %get-tuple-element.19) | copy-start | bytes 786436
  61.1 8.3 %collective-permute-start.4 = (bf16[1,1,128,512]{3,2,1,0:T(8,128)(2,1)S(1)}, bf16[1,1,128,512]{3,2,1,0:T(8,128)(2,1)S(1)}, u32[]{:S(2)}, u32[]{:S(2)}) collective-permute-start(bf16[1,1,128,512]{3,2,1,0:T(8,128)(2,1)S(1)} %slice_bitcast_fusion.6), channel_id=1, source_target_pairs={{0,4},{4,8},{8,12},{12,0},{1,5},{5,9},{9,13},{13,1},{2,6},{6,10},{... | collective-permute-start | bytes 393224 | tf_op jit(solution)/shard_map/ppermute | solution.py:14
  62.9 7.6 %collective-permute-start.5 = (bf16[1,1,128,512]{3,2,1,0:T(8,128)(2,1)S(1)}, bf16[1,1,128,512]{3,2,1,0:T(8,128)(2,1)S(1)}, u32[]{:S(2)}, u32[]{:S(2)}) collective-permute-start(bf16[1,1,128,512]{3,2,1,0:T(8,128)(2,1)S(1)} %slice_bitcast_fusion.6), channel_id=1, source_target_pairs={{4,0},{8,4},{12,8},{0,12},{5,1},{9,5},{13,9},{1,13},{6,2},{10,6},{... | collective-permute-start | bytes 393224 | tf_op jit(solution)/shard_map/ppermute | solution.py:17
  70.5 12.1 %collective-permute-start.6 = (bf16[3,1,128,512]{3,2,1,0:T(8,128)(2,1)S(1)}, bf16[3,1,128,512]{3,2,1,0:T(8,128)(2,1)S(1)}, u32[]{:S(2)}, u32[]{:S(2)}) collective-permute-start(bf16[3,1,128,512]{3,2,1,0:T(8,128)(2,1)S(1)} %pad_maximum_fusion.2), channel_id=1, source_target_pairs={{0,2},{2,0},{1,3},{3,1},{4,6},{6,4},{5,7},{7,5},{8,10},{10,8},{9,1... | collective-permute-start | bytes 1179656 | tf_op jit(solution)/shard_map/ppermute | solution.py:14
  72.0 17.5 %collective-permute-start.7 = (bf16[3,1,128,512]{3,2,1,0:T(8,128)(2,1)S(1)}, bf16[3,1,128,512]{3,2,1,0:T(8,128)(2,1)S(1)}, u32[]{:S(2)}, u32[]{:S(2)}) collective-permute-start(bf16[3,1,128,512]{3,2,1,0:T(8,128)(2,1)S(1)} %pad_maximum_fusion.2), channel_id=1, source_target_pairs={{2,0},{0,2},{3,1},{1,3},{6,4},{4,6},{7,5},{5,7},{10,8},{8,10},{11,... | collective-permute-start | bytes 1179656 | tf_op jit(solution)/shard_map/ppermute | solution.py:17
  101.8 70.0 %reduce-scatter.8.cloned.1.call-start = ((), (), s32[]{:S(2)}) async-start(), calls=%async_computation.5 | async-start | bytes 1310720 | tf_op jit(solution)/shard_map/reduce_scatter | solution.py:121
  103.7 5.6 %copy-start.3 = (bf16[256,512]{1,0:T(8,128)(2,1)S(1)}, bf16[256,512]{1,0:T(8,128)(2,1)}, u32[]{:S(2)}) copy-start(bf16[256,512]{1,0:T(8,128)(2,1)} %copy-done.2) | copy-start | bytes 786436
  103.7 5.6 %copy-start.17 = (f32[256]{0:T(256)S(1)}, f32[256]{0:T(256)}, u32[]{:S(2)}) copy-start(f32[256]{0:T(256)} %compare_convert_fusion.1) | copy-start | bytes 3076
  103.7 5.6 %copy-start.19 = (bf16[1,1,256,512]{3,2,1,0:T(8,128)(2,1)S(1)}, bf16[1,1,256,512]{3,2,1,0:T(8,128)(2,1)}, u32[]{:S(2)}) copy-start(bf16[1,1,256,512]{3,2,1,0:T(8,128)(2,1)} %param.11) | copy-start | bytes 786436
  105.2 6.4 %copy-start.7 = (bf16[2,512,512]{2,1,0:T(8,128)(2,1)S(1)}, bf16[2,512,512]{2,1,0:T(8,128)(2,1)}, u32[]{:S(2)}) copy-start(bf16[2,512,512]{2,1,0:T(8,128)(2,1)} %multiply_convert_fusion) | copy-start | bytes 3145732
  127.3 9.1 %copy-start.1 = (f32[512,512]{1,0:T(8,128)S(1)}, f32[512,512]{1,0:T(8,128)}, u32[]{:S(2)}) copy-start(f32[512,512]{1,0:T(8,128)} %squeeze.39) | copy-start | bytes 3145732
  127.3 9.1 %copy-start.4 = (bf16[256,512]{1,0:T(8,128)(2,1)S(1)}, bf16[256,512]{1,0:T(8,128)(2,1)}, u32[]{:S(2)}) copy-start(bf16[256,512]{1,0:T(8,128)(2,1)} %copy-done.2) | copy-start | bytes 786436
  127.3 9.1 %copy-start.11 = (bf16[256,512]{1,0:T(8,128)(2,1)S(1)}, bf16[256,512]{1,0:T(8,128)(2,1)}, u32[]{:S(2)}) copy-start(bf16[256,512]{1,0:T(8,128)(2,1)} %reduce-scatter.6.cloned.1.call-done) | copy-start | bytes 786436
  127.3 9.0 %copy-start.13 = (bf16[256,512]{1,0:T(8,128)(2,1)S(1)}, bf16[256,512]{1,0:T(8,128)(2,1)}, u32[]{:S(2)}) copy-start(bf16[256,512]{1,0:T(8,128)(2,1)} %copy-done.12) | copy-start | bytes 786436
  127.4 9.4 %collective-permute-start.10 = (bf16[1,128,512]{2,1,0:T(8,128)(2,1)S(1)}, bf16[1,128,512]{2,1,0:T(8,128)(2,1)S(1)}, u32[]{:S(2)}, u32[]{:S(2)}) collective-permute-start(bf16[1,128,512]{2,1,0:T(8,128)(2,1)S(1)} %get-tuple-element.9), channel_id=1, source_target_pairs={{0,2},{1,3},{4,6},{5,7},{8,10},{9,11},{12,14},{13,15},{16,18},{17,... | collective-permute-start | bytes 393224 | tf_op jit(solution)/shard_map/ppermute | solution.py:14
  131.1 7.3 %collective-permute-start.11 = (bf16[1,128,512]{2,1,0:T(8,128)(2,1)S(1)}, bf16[1,128,512]{2,1,0:T(8,128)(2,1)S(1)}, u32[]{:S(2)}, u32[]{:S(2)}) collective-permute-start(bf16[1,128,512]{2,1,0:T(8,128)(2,1)S(1)} %get-tuple-element.8), channel_id=1, source_target_pairs={{2,0},{3,1},{6,4},{7,5},{10,8},{11,9},{14,12},{15,13},{18,16},{19,... | collective-permute-start | bytes 393224 | tf_op jit(solution)/shard_map/ppermute | solution.py:17
  132.4 8.2 %collective-permute-start.8 = (bf16[1,128,512]{2,1,0:T(8,128)(2,1)S(1)}, bf16[1,128,512]{2,1,0:T(8,128)(2,1)S(1)}, u32[]{:S(2)}, u32[]{:S(2)}) collective-permute-start(bf16[1,128,512]{2,1,0:T(8,128)(2,1)S(1)} %get-tuple-element.7), channel_id=1, source_target_pairs={{0,4},{4,8},{8,12},{12,0},{1,5},{5,9},{9,13},{13,1},{2,6},{6,10},{... | collective-permute-start | bytes 393224 | tf_op jit(solution)/shard_map/ppermute | solution.py:14
  134.0 8.0 %collective-permute-start.9 = (bf16[1,128,512]{2,1,0:T(8,128)(2,1)S(1)}, bf16[1,128,512]{2,1,0:T(8,128)(2,1)S(1)}, u32[]{:S(2)}, u32[]{:S(2)}) collective-permute-start(bf16[1,128,512]{2,1,0:T(8,128)(2,1)S(1)} %get-tuple-element.10), channel_id=1, source_target_pairs={{4,0},{8,4},{12,8},{0,12},{5,1},{9,5},{13,9},{1,13},{6,2},{10,6},{... | collective-permute-start | bytes 393224 | tf_op jit(solution)/shard_map/ppermute | solution.py:17
  136.3 5.7 %copy-start.22 = (f32[256,512]{1,0:T(8,128)S(1)}, f32[256,512]{1,0:T(8,128)}, u32[]{:S(2)}) copy-start(f32[256,512]{1,0:T(8,128)} %get-tuple-element.20) | copy-start | bytes 1572868
  136.7 5.4 %copy-start.5 = (f32[512,512]{1,0:T(8,128)S(1)}, f32[512,512]{1,0:T(8,128)}, u32[]{:S(2)}) copy-start(f32[512,512]{1,0:T(8,128)} %squeeze.38) | copy-start | bytes 3145732
  136.7 5.4 %copy-start.8 = (bf16[1,1,256,512]{3,2,1,0:T(8,128)(2,1)S(1)}, bf16[1,1,256,512]{3,2,1,0:T(8,128)(2,1)}, u32[]{:S(2)}) copy-start(bf16[1,1,256,512]{3,2,1,0:T(8,128)(2,1)} %param.10) | copy-start | bytes 786436
  136.7 5.4 %copy-start.10 = (bf16[256,512]{1,0:T(8,128)(2,1)S(1)}, bf16[256,512]{1,0:T(8,128)(2,1)}, u32[]{:S(2)}) copy-start(bf16[256,512]{1,0:T(8,128)(2,1)} %copy-done.9) | copy-start | bytes 786436
  136.7 5.4 %copy-start.20 = (bf16[1,1,256,512]{3,2,1,0:T(8,128)(2,1)S(1)}, bf16[1,1,256,512]{3,2,1,0:T(8,128)(2,1)}, u32[]{:S(2)}) copy-start(bf16[1,1,256,512]{3,2,1,0:T(8,128)(2,1)} %param.11) | copy-start | bytes 786436
  143.8 44.8 %all-gather.3.cloned.1.call-start = ((), (), s32[]{:S(2)}) async-start(), calls=%async_computation.6 | async-start | bytes 1310720 | tf_op jit(solution)/shard_map/all_gather | solution.py:122
  (7 other events, 24.0 us)
Sparse Core Ops, SparseCore 0:
  50.3 7.6 reduce-scatter.3
  101.9 7.3 reduce-scatter.5
  143.9 27.7 reduce-scatter.7
  173.2 15.3 all-gather.2
